TPU v7x, 512 devices: a whole 4x4x16 slice. The times are simulated.
512 devices in a mesh: rows: 64 (over x, z), cols: 8 (over y, core).
Axes of the slice: x: 4, y: 4, z: 16, core: 2. Of those that a mesh axis runs over, the one named last changes fastest.
Arguments:
- sketch: bfloat16 [131072, 256], P(('rows', 'cols')), may hold values from -6 to 6
- blocks: bfloat16 [4096, 256, 256], P(('rows', 'cols')), may hold values from -0.375 to 0.375
- block_rows: int32 [4096], P(('rows', 'cols')), may hold values from 0 to 3, as said below
- block_cols: int32 [4096], P(('rows', 'cols')), may hold values from 0 to 63
- counts: int32 [512], P(('rows', 'cols')), may hold values from 1 to 8, as said below
Outputs:
- basis: float32 [65536, 256], P(('rows', 'cols'))
- factor: float32 [256, 256], replicated
Inputs may be any that keep to these rules, and one draw needn't show every extreme that they name: Within one device's 8 slots the pairs (block_rows, block_cols) are distinct. `counts`: some device has exactly 8 live slots.
All inputs are finite; a program needn't handle non-finite values.
Results may differ from a plain program's by a relative error of at most 0.0003.
Values may be sent and summed in bfloat16 or wider, within the bound.
A program may use at most 64 MiB of HBM per device.

v0:
```python
import jax
import jax.numpy as jnp
from jax import lax
from jax.sharding import PartitionSpec as P

RB = 4


def local(sketch, blocks, block_rows, block_cols, counts):
    highest = lax.Precision.HIGHEST
    slots, width, _ = blocks.shape
    columns = sketch.shape[1]
    live_count = counts[0]
    starts = block_cols * width
    panel = lax.all_gather(sketch, "rows", axis=0, tiled=True)
    chosen = jax.vmap(lambda offset: lax.dynamic_slice_in_dim(panel, offset, width, 0))(starts)
    products = jnp.einsum("bij,bjk->bik", blocks, chosen, preferred_element_type=jnp.float32)
    selector = (
        (block_rows[:, None] == jnp.arange(RB, dtype=jnp.int32)[None, :])
        & (jnp.arange(slots, dtype=jnp.int32) < live_count)[:, None]
    ).astype(jnp.float32)
    partial_rows = jnp.einsum("br,bik->rik", selector, products, precision=highest)
    partial_rows = partial_rows.reshape(RB * width, columns)
    total_rows = RB * width * lax.axis_size("rows")
    slab_total = lax.psum(partial_rows, "cols")
    gram_matrix = lax.psum(jnp.dot(slab_total.T, slab_total, precision=highest), "rows")
    share_rows = slab_total.shape[0] // lax.axis_size("cols")
    own_rows = lax.dynamic_slice_in_dim(
        slab_total, lax.axis_index("cols") * share_rows, share_rows, 0
    )
    lower_factor = jnp.linalg.cholesky(gram_matrix)
    root_rows = jnp.sqrt(jnp.float32(total_rows))
    solved = lax.linalg.triangular_solve(
        lower_factor, own_rows, left_side=False, lower=True, transpose_a=True
    )
    return (solved * root_rows, lower_factor.T / root_rows)


def solution(mesh):
    in_specs = (
        P(("rows", "cols"), None),
        P(("rows", "cols"), None, None),
        P(("rows", "cols")),
        P(("rows", "cols")),
        P(("rows", "cols")),
    )
    out_specs = (P(("rows", "cols"), None), P())
    return jax.shard_map(local, mesh=mesh, in_specs=in_specs, out_specs=out_specs, check_vma=False)
```

profile of v0, /device:TPU:8, one launch (start us, length us, event | category | flops | bytes accessed | tf_op | source)
XLA Modules:
  0.0 611.1 jit_solution(694707326038857665)
XLA Ops:
  7.2 0.7 all-gather.2.cloned.1.call-update
  8.0 0.7 fusion.16
  9.3 162.0 %all-gather.2.cloned.1.call-done = bf16[16384,256]{1,0:T(8,128)(2,1)} async-done(((bf16[256,256]{1,0:T(8,128)(2,1)}), bf16[16384,256]{1,0:T(8,128)(2,1)}) %all-gather.2.cloned.1.call-update) | async-done | bytes 8388624 | tf_op jit(solution)/shard_map/all_gather | solution.py:15
  171.3 17.0 %while.2 = (s32[]{:T(128)}, bf16[16384,256]{1,0:T(8,128)(2,1)}, s32[8,2]{0,1:T(2,128)S(1)}, bf16[8,256,256]{2,1,0:T(8,128)(2,1)S(1)}, s32[]{:T(128)}) while((s32[]{:T(128)}, bf16[16384,256]{1,0:T(8,128)(2,1)}, s32[8,2]{0,1:T(2,128)S(1)}, bf16[8,256,256]{2,1,0:T(8,128)(2,1)S(1)}, s32[]{:T(128)}) %tuple.41), condition=%wide.while_cond, body=%wide.while_body.sunk | while | flops 2 | bytes 262241 | solution.py:16
  171.4 0.5 slice.69
  171.9 1.5 bitcast_dynamic-update-slice_fusion.4
  173.5 0.5 slice.69
  174.0 1.5 bitcast_dynamic-update-slice_fusion.4
  175.7 0.5 slice.69
  176.2 1.5 bitcast_dynamic-update-slice_fusion.4
  177.8 0.5 slice.69
  178.3 1.5 bitcast_dynamic-update-slice_fusion.4
  179.9 0.5 slice.69
  180.4 1.5 bitcast_dynamic-update-slice_fusion.4
  182.0 0.5 slice.69
  182.6 1.5 bitcast_dynamic-update-slice_fusion.4
  184.1 0.1 constant_dynamic-slice_fusion.4
  184.2 0.5 slice.69
  184.7 1.5 bitcast_dynamic-update-slice_fusion.4
  186.3 0.5 slice.69
  186.8 1.5 bitcast_dynamic-update-slice_fusion.4
  188.4 1.8 fusion.19
  190.2 2.2 copy.16
  192.4 1.1 fusion
  193.5 1.2 copy.11
  194.8 0.2 all-reduce.7.cloned.1.call-start
  195.0 70.9 %all-reduce.5.cloned.1.call-done = f32[1024,256]{1,0:T(8,128)} async-done(((f32[1024,256]{1,0:T(8,128)}), f32[1024,256]{1,0:T(8,128)}) %all-reduce.5.cloned.1.call-update) | async-done | bytes 1048592 | tf_op jit(solution)/shard_map/psum | solution.py:25
  265.9 4.1 fusion.20
  270.0 268.6 %all-reduce.7.cloned.1.call-done = f32[256,256]{0,1:T(8,128)} async-done(((f32[256,256]{0,1:T(8,128)}), f32[256,256]{0,1:T(8,128)}) %all-reduce.7.cloned.1.call-update) | async-done | bytes 262160 | tf_op jit(solution)/shard_map/psum | solution.py:26
  538.6 1.1 copy.13
  539.6 1.0 fusion.2
  540.6 11.7 %cholesky.50 = f32[128,128]{1,0:T(8,128)S(1)} custom-call(f32[128,128]{1,0:T(8,128)S(1)} %cholesky.118), custom_call_target="Cholesky" | custom-call | tf_op jit(solution)/shard_map/jit(cholesky)/cholesky | solution.py:31
  552.4 9.8 %custom-call.14 = f32[1,128,128]{1,2,0:T(8,128)S(1)} custom-call(f32[1,128,128]{2,1,0:T(8,128)S(1)} %get-tuple-element.45), custom_call_target="InvertDiagBlocksLowerTriangular" | custom-call | tf_op jit(solution)/shard_map/jit(cholesky)/cholesky | solution.py:31
  562.2 0.2 constant_dynamic-update-slice_fusion.1
  562.5 0.3 convolution_subtract_fusion.1
  562.7 11.7 %cholesky.105 = f32[128,128]{1,0:T(8,128)S(1)} custom-call(f32[128,128]{1,0:T(8,128)S(1)} %convolution_subtract_fusion.1), custom_call_target="Cholesky" | custom-call | tf_op jit(solution)/shard_map/jit(cholesky)/cholesky | solution.py:31
  574.5 0.8 compare_reduce_fusion
  576.7 4.0 while.3
  576.7 0.6 fusion.30
  577.3 1.4 bitcast_dynamic-update-slice_fusion.5
  578.7 0.6 fusion.30
  579.3 1.4 bitcast_dynamic-update-slice_fusion.5
  580.7 19.7 %custom-call.15 = f32[2,128,128]{1,2,0:T(8,128)S(1)} custom-call(f32[2,128,128]{2,1,0:T(8,128)S(1)} %get-tuple-element.17), custom_call_target="InvertDiagBlocksLowerTriangular" | custom-call | tf_op jit(solution)/shard_map/triangular_solve | solution.py:33
  600.4 1.1 fusion.6
  601.5 1.1 convolution_subtract_fusion
  602.7 0.3 fusion.4
  603.0 0.8 copy.14
  603.7 0.8 copy.15
  (29 shorter events, 0.9 us)
Async XLA Ops:
  7.2 181.2 %copy-start = (bf16[8,256,256]{2,1,0:T(8,128)(2,1)S(1)}, bf16[8,256,256]{2,1,0:T(8,128)(2,1)}, u32[]{:S(2)}) copy-start(bf16[8,256,256]{2,1,0:T(8,128)(2,1)} %param.6) | copy-start | bytes 3145732
  7.2 164.1 %all-gather.2.cloned.1.call-start = ((), (), s32[]{:S(2)}) async-start(), calls=%async_computation | async-start | bytes 8519680 | tf_op jit(solution)/shard_map/all_gather | solution.py:15
  7.9 258.0 %all-reduce.5.cloned.1.call-start = ((), (), s32[]{:S(2)}) async-start(), calls=%async_computation.1 | async-start | bytes 2097152 | tf_op jit(solution)/shard_map/psum | solution.py:25
  190.2 2.2 copy-start.1
  194.8 343.8 %all-reduce.7.cloned.1.call-start = ((), (), s32[]{:S(2)}) async-start(), calls=%async_computation.2 | async-start | bytes 524288 | tf_op jit(solution)/shard_map/psum | solution.py:26
Sparse Core Ops, SparseCore 0:
  10.9 160.3 all-gather.1
  194.9 70.9 all-reduce.4
  270.1 268.4 all-reduce.6
where the time goes:
time: 612 us; the launch traced here: 611 us
  waiting for transfers between devices  502 us (82%)
  other arithmetic  55.5 us (9%)
  local copies, waits for them, and re-layouts  27 us (4%)
  between operations  15.9 us (3%)
  matrix products  10 us (2%)
    psum x1, waiting for transfers between devices, local(): lax.psum(jnp.dot(slab_total.T, slab_total, precision=highest), 'rows')  269 us
    all_gather x1, waiting for transfers between devices, local(): panel = lax.all_gather(sketch, 'rows', axis=0, tiled=True)  162 us
    psum x1, waiting for transfers between devices, local(): slab_total = lax.psum(partial_rows, 'cols')  70.9 us
    another operation x6, other arithmetic, local(): lower_factor = jnp.linalg.cholesky(gram_matrix)  34.2 us
    another operation x2, other arithmetic, local(): lax.linalg.triangular_solve(lower_factor, own_rows, left_side=False, lowe...  19.7 us
    gather x24, local copies, waits for them, and re-layouts  16.9 us
  transfers between devices with their start and end apart: 3, of which 3 were waited for; matrix products, arithmetic and copies ran while one was open for 0% of the time, Pallas kernels for 0%

commit v1 on v0

--- a/solution.py
+++ b/solution.py
@@ -12,7 +12,9 @@
     columns = sketch.shape[1]
     live_count = counts[0]
     starts = block_cols * width
-    panel = lax.all_gather(sketch, "rows", axis=0, tiled=True)
+    panel = jnp.concatenate(
+        lax.all_to_all(jnp.stack([sketch] * lax.axis_size("rows")), "rows", 0, 0), axis=0
+    )
     chosen = jax.vmap(lambda offset: lax.dynamic_slice_in_dim(panel, offset, width, 0))(starts)
     products = jnp.einsum("bij,bjk->bik", blocks, chosen, preferred_element_type=jnp.float32)
     selector = (

time: 612 us -> 838 us (1.37)
  waiting for transfers between devices: 502 us -> 705 us
  starting transfers between devices: 0.3 us -> 19.2 us
    all_to_all x0 -> x1, waiting for transfers between devices: none -> 367 us  [local(): lax.all_to_all(jnp.stack([sketch] * lax.axis_size('rows')), 'rows', 0, 0)]
    all_gather x1 -> x0, waiting for transfers between devices: 162 us -> none  [local(): panel = lax.all_gather(sketch, 'rows', axis=0, tiled=True)]
    all_to_all x0 -> x1, starting transfers between devices: none -> 19 us  [local(): lax.all_to_all(jnp.stack([sketch] * lax.axis_size('rows')), 'rows', 0, 0)]
where the time goes in v1:
time: 838 us; the launch traced here: 837 us
  waiting for transfers between devices  705 us (84%)
  other arithmetic  54.9 us (7%)
  local copies, waits for them, and re-layouts  32.3 us (4%)
  starting transfers between devices  19.2 us (2%)
  between operations  16.2 us (2%)
  matrix products  10 us (1%)
    all_to_all x1, waiting for transfers between devices, local(): lax.all_to_all(jnp.stack([sketch] * lax.axis_size('rows')), 'rows', 0, 0)  367 us
    psum x1, waiting for transfers between devices, local(): lax.psum(jnp.dot(slab_total.T, slab_total, precision=highest), 'rows')  269 us
    psum x1, waiting for transfers between devices, local(): slab_total = lax.psum(partial_rows, 'cols')  69.2 us
    another operation x6, other arithmetic, local(): lower_factor = jnp.linalg.cholesky(gram_matrix)  34.2 us
    another operation x2, other arithmetic, local(): lax.linalg.triangular_solve(lower_factor, own_rows, left_side=False, lowe...  19.7 us
    all_to_all x1, starting transfers between devices, local(): lax.all_to_all(jnp.stack([sketch] * lax.axis_size('rows')), 'rows', 0, 0)  19 us
    gather x24, local copies, waits for them, and re-layouts  16.9 us
  transfers between devices with their start and end apart: 3, of which 3 were waited for; matrix products, arithmetic and copies ran while one was open for 0% of the time, Pallas kernels for 0%

profile of v1, /device:TPU:8, one launch (start us, length us, event | category | flops | bytes accessed | tf_op | source)
XLA Modules:
  0.0 837.3 jit_solution(13469405474299308735)
XLA Ops:
  7.2 5.2 stack.2
  12.4 19.0 %all-to-all-start = ((bf16[64,256,256]{2,1,0:T(8,128)(2,1)}), bf16[64,256,256]{2,1,0:T(8,128)(2,1)}, u32[]{:S(2)}, u32[]{:S(2)}) async-start(bf16[64,256,256]{2,1,0:T(8,128)(2,1)} %stack.2), calls=%async_computation | async-start | bytes 16777216 | tf_op jit(solution)/shard_map/all_to_all | solution.py:16
  32.1 366.8 %all-to-all-done = bf16[64,256,256]{2,1,0:T(8,128)(2,1)} async-done(((bf16[64,256,256]{2,1,0:T(8,128)(2,1)}), bf16[64,256,256]{2,1,0:T(8,128)(2,1)}, u32[]{:S(2)}, u32[]{:S(2)}) %all-to-all-start) | async-done | bytes 8388640 | tf_op jit(solution)/shard_map/all_to_all | solution.py:16
  399.0 17.0 %while.2 = (s32[]{:T(128)}, bf16[16384,256]{1,0:T(8,128)(2,1)}, s32[8,2]{0,1:T(2,128)S(1)}, bf16[8,256,256]{2,1,0:T(8,128)(2,1)S(1)}, s32[]{:T(128)}) while((s32[]{:T(128)}, bf16[16384,256]{1,0:T(8,128)(2,1)}, s32[8,2]{0,1:T(2,128)S(1)}, bf16[8,256,256]{2,1,0:T(8,128)(2,1)S(1)}, s32[]{:T(128)}) %tuple.41), condition=%wide.while_cond, body=%wide.while_body.sunk | while | flops 2 | bytes 262241 | solution.py:18
  399.0 0.5 slice.69
  399.5 1.5 bitcast_dynamic-update-slice_fusion.4
  401.1 0.1 constant_dynamic-slice_fusion.4
  401.2 0.5 slice.69
  401.7 1.5 bitcast_dynamic-update-slice_fusion.4
  403.3 0.5 slice.69
  403.8 1.5 bitcast_dynamic-update-slice_fusion.4
  405.4 0.5 slice.69
  405.9 1.5 bitcast_dynamic-update-slice_fusion.4
  407.6 0.5 slice.69
  408.1 1.5 bitcast_dynamic-update-slice_fusion.4
  409.7 0.5 slice.69
  410.2 1.5 bitcast_dynamic-update-slice_fusion.4
  411.8 0.5 slice.69
  412.3 1.5 bitcast_dynamic-update-slice_fusion.4
  413.9 0.5 slice.69
  414.5 1.5 bitcast_dynamic-update-slice_fusion.4
  416.0 1.8 fusion.19
  417.8 2.2 copy.16
  420.1 1.1 fusion
  421.2 1.2 copy.11
  422.4 0.2 all-reduce.7.cloned.1.call-start
  422.6 69.2 %all-reduce.5.cloned.1.call-done = f32[1024,256]{1,0:T(8,128)} async-done(((f32[1024,256]{1,0:T(8,128)}), f32[1024,256]{1,0:T(8,128)}) %all-reduce.5.cloned.1.call-update) | async-done | bytes 1048592 | tf_op jit(solution)/shard_map/psum | solution.py:27
  491.8 4.1 fusion.20
  495.9 268.6 %all-reduce.7.cloned.1.call-done = f32[256,256]{0,1:T(8,128)} async-done(((f32[256,256]{0,1:T(8,128)}), f32[256,256]{0,1:T(8,128)}) %all-reduce.7.cloned.1.call-update) | async-done | bytes 262160 | tf_op jit(solution)/shard_map/psum | solution.py:28
  764.5 1.1 copy.13
  765.6 1.0 fusion.2
  766.6 11.7 %cholesky.50 = f32[128,128]{1,0:T(8,128)S(1)} custom-call(f32[128,128]{1,0:T(8,128)S(1)} %cholesky.118), custom_call_target="Cholesky" | custom-call | tf_op jit(solution)/shard_map/jit(cholesky)/cholesky | solution.py:33
  778.3 9.8 %custom-call.14 = f32[1,128,128]{1,2,0:T(8,128)S(1)} custom-call(f32[1,128,128]{2,1,0:T(8,128)S(1)} %get-tuple-element.45), custom_call_target="InvertDiagBlocksLowerTriangular" | custom-call | tf_op jit(solution)/shard_map/jit(cholesky)/cholesky | solution.py:33
  788.2 0.2 constant_dynamic-update-slice_fusion.1
  788.4 0.3 convolution_subtract_fusion.1
  788.6 11.7 %cholesky.105 = f32[128,128]{1,0:T(8,128)S(1)} custom-call(f32[128,128]{1,0:T(8,128)S(1)} %convolution_subtract_fusion.1), custom_call_target="Cholesky" | custom-call | tf_op jit(solution)/shard_map/jit(cholesky)/cholesky | solution.py:33
  800.4 0.8 compare_reduce_fusion
  802.6 4.0 while.3
  802.6 0.6 fusion.30
  803.2 1.4 bitcast_dynamic-update-slice_fusion.5
  804.6 0.6 fusion.30
  805.2 1.4 bitcast_dynamic-update-slice_fusion.5
  806.6 19.7 %custom-call.15 = f32[2,128,128]{1,2,0:T(8,128)S(1)} custom-call(f32[2,128,128]{2,1,0:T(8,128)S(1)} %get-tuple-element.17), custom_call_target="InvertDiagBlocksLowerTriangular" | custom-call | tf_op jit(solution)/shard_map/triangular_solve | solution.py:35
  826.3 1.1 fusion.6
  827.4 1.1 convolution_subtract_fusion
  828.6 0.3 fusion.4
  828.9 0.8 copy.14
  829.6 0.8 copy.15
  (31 shorter events, 0.9 us)
Async XLA Ops:
  7.2 408.8 %copy-start = (bf16[8,256,256]{2,1,0:T(8,128)(2,1)S(1)}, bf16[8,256,256]{2,1,0:T(8,128)(2,1)}, u32[]{:S(2)}) copy-start(bf16[8,256,256]{2,1,0:T(8,128)(2,1)} %param.6) | copy-start | bytes 3145732
  12.4 19.0 %copy-start.2 = (s32[8]{0:T(128)S(1)}, s32[8]{0:T(128)}, u32[]{:S(2)}) copy-start(s32[8]{0:T(128)} %param.8) | copy-start | bytes 100
  12.4 386.6 %all-to-all-start = ((bf16[64,256,256]{2,1,0:T(8,128)(2,1)}), bf16[64,256,256]{2,1,0:T(8,128)(2,1)}, u32[]{:S(2)}, u32[]{:S(2)}) async-start(bf16[64,256,256]{2,1,0:T(8,128)(2,1)} %stack.2), calls=%async_computation | async-start | bytes 16777216 | tf_op jit(solution)/shard_map/all_to_all | solution.py:16
  31.4 460.4 %all-reduce.5.cloned.1.call-start = ((), (), s32[]{:S(2)}) async-start(), calls=%async_computation.1 | async-start | bytes 2097152 | tf_op jit(solution)/shard_map/psum | solution.py:27
  417.8 2.2 copy-start.1
  422.4 342.1 %all-reduce.7.cloned.1.call-start = ((), (), s32[]{:S(2)}) async-start(), calls=%async_computation.2 | async-start | bytes 524288 | tf_op jit(solution)/shard_map/psum | solution.py:28
Sparse Core Ops, SparseCore 0:
  422.5 69.2 all-reduce.4
  496.0 268.4 all-reduce.6

commit v2 on v0

--- a/solution.py
+++ b/solution.py
@@ -22,7 +22,7 @@
     partial_rows = jnp.einsum("br,bik->rik", selector, products, precision=highest)
     partial_rows = partial_rows.reshape(RB * width, columns)
     total_rows = RB * width * lax.axis_size("rows")
-    slab_total = lax.psum(partial_rows, "cols")
+    slab_total = jnp.sum(lax.all_gather(partial_rows, "cols"), axis=0)
     gram_matrix = lax.psum(jnp.dot(slab_total.T, slab_total, precision=highest), "rows")
     share_rows = slab_total.shape[0] // lax.axis_size("cols")
     own_rows = lax.dynamic_slice_in_dim(

time: 612 us -> 592 us (0.967)
  waiting for transfers between devices: 502 us -> 482 us
    psum x1 -> x0, waiting for transfers between devices: 70.9 us -> none  [local(): slab_total = lax.psum(partial_rows, 'cols')]
    all_gather x0 -> x1, waiting for transfers between devices: none -> 51.5 us  [local(): slab_total = jnp.sum(lax.all_gather(partial_rows, 'cols'), axis=0)]
where the time goes in v2:
time: 592 us
  waiting for transfers between devices  482 us (81%)
  other arithmetic  59.6 us (10%)
  local copies, waits for them, and re-layouts  27.1 us (5%)
  between operations  15.9 us (3%)
  matrix products  6.78 us (1%)
    psum x1, waiting for transfers between devices, local(): lax.psum(jnp.dot(slab_total.T, slab_total, precision=highest), 'rows')  268 us
    all_gather x1, waiting for transfers between devices, local(): panel = lax.all_gather(sketch, 'rows', axis=0, tiled=True)  162 us
    all_gather x1, waiting for transfers between devices, local(): slab_total = jnp.sum(lax.all_gather(partial_rows, 'cols'), axis=0)  51.5 us
    another operation x6, other arithmetic, local(): lower_factor = jnp.linalg.cholesky(gram_matrix)  34.2 us
    another operation x2, other arithmetic, local(): lax.linalg.triangular_solve(lower_factor, own_rows, left_side=False, lowe...  19.7 us
    gather x24, local copies, waits for them, and re-layouts  16.9 us
  transfers between devices with their start and end apart: 3, of which 3 were waited for; matrix products, arithmetic and copies ran while one was open for 0% of the time, Pallas kernels for 0%

profile of v2, /device:TPU:8, one launch (start us, length us, event | category | flops | bytes accessed | tf_op | source)
XLA Modules:
  0.0 592.0 jit_solution(18172097485865483841)
XLA Ops:
  7.2 0.7 all-gather.3.cloned.1.call-update
  8.0 0.7 fusion.15
  9.3 162.0 %all-gather.3.cloned.1.call-done = bf16[16384,256]{1,0:T(8,128)(2,1)} async-done(((bf16[256,256]{1,0:T(8,128)(2,1)}), bf16[16384,256]{1,0:T(8,128)(2,1)}) %all-gather.3.cloned.1.call-update) | async-done | bytes 8388624 | tf_op jit(solution)/shard_map/all_gather | solution.py:15
  171.3 17.0 %while.2 = (s32[]{:T(128)}, bf16[16384,256]{1,0:T(8,128)(2,1)}, s32[8,2]{0,1:T(2,128)S(1)}, bf16[8,256,256]{2,1,0:T(8,128)(2,1)S(1)}, s32[]{:T(128)}) while((s32[]{:T(128)}, bf16[16384,256]{1,0:T(8,128)(2,1)}, s32[8,2]{0,1:T(2,128)S(1)}, bf16[8,256,256]{2,1,0:T(8,128)(2,1)S(1)}, s32[]{:T(128)}) %tuple.42), condition=%wide.while_cond, body=%wide.while_body.sunk | while | flops 2 | bytes 262241 | solution.py:16
  171.4 0.5 slice.69
  171.9 1.5 bitcast_dynamic-update-slice_fusion.4
  173.5 0.5 slice.69
  174.0 1.5 bitcast_dynamic-update-slice_fusion.4
  175.7 0.5 slice.69
  176.2 1.5 bitcast_dynamic-update-slice_fusion.4
  177.8 0.5 slice.69
  178.3 1.5 bitcast_dynamic-update-slice_fusion.4
  179.9 0.5 slice.69
  180.4 1.5 bitcast_dynamic-update-slice_fusion.4
  182.0 0.5 slice.69
  182.6 1.5 bitcast_dynamic-update-slice_fusion.4
  184.2 0.5 slice.69
  184.7 1.5 bitcast_dynamic-update-slice_fusion.4
  186.3 0.5 slice.69
  186.8 1.5 bitcast_dynamic-update-slice_fusion.4
  188.4 1.8 convolution_bitcast_fusion
  190.2 2.2 copy.17
  192.4 1.1 fusion.11
  193.5 1.2 copy.18
  194.8 0.2 all-reduce.4.cloned.1.call-start
  195.0 51.5 %all-gather.5.cloned.1.call-done = f32[8,1024,256]{2,1,0:T(8,128)} async-done(((f32[1,1024,256]{2,1,0:T(8,128)}), f32[8,1024,256]{2,1,0:T(8,128)}) %all-gather.5.cloned.1.call-update) | async-done | bytes 8388624 | tf_op jit(solution)/shard_map/all_gather | solution.py:25
  246.5 4.1 reduce_sum.9
  250.6 2.5 fusion.18
  253.2 267.9 %all-reduce.4.cloned.1.call-done = f32[256,256]{0,1:T(8,128)} async-done(((f32[256,256]{0,1:T(8,128)}), f32[256,256]{0,1:T(8,128)}) %all-reduce.4.cloned.1.call-update) | async-done | bytes 262160 | tf_op jit(solution)/shard_map/psum | solution.py:26
  521.1 1.1 copy.20
  522.2 1.0 fusion
  523.2 11.7 %cholesky.50 = f32[128,128]{1,0:T(8,128)S(1)} custom-call(f32[128,128]{1,0:T(8,128)S(1)} %cholesky.118), custom_call_target="Cholesky" | custom-call | tf_op jit(solution)/shard_map/jit(cholesky)/cholesky | solution.py:31
  535.0 9.8 %custom-call.14 = f32[1,128,128]{1,2,0:T(8,128)S(1)} custom-call(f32[1,128,128]{2,1,0:T(8,128)S(1)} %get-tuple-element.47), custom_call_target="InvertDiagBlocksLowerTriangular" | custom-call | tf_op jit(solution)/shard_map/jit(cholesky)/cholesky | solution.py:31
  544.8 0.2 constant_dynamic-update-slice_fusion.1
  545.0 0.3 convolution_subtract_fusion.1
  545.3 11.9 %cholesky.105 = f32[128,128]{1,0:T(8,128)S(1)} custom-call(f32[128,128]{1,0:T(8,128)S(1)} %convolution_subtract_fusion.1), custom_call_target="Cholesky" | custom-call | tf_op jit(solution)/shard_map/jit(cholesky)/cholesky | solution.py:31
  557.2 0.7 compare_reduce_fusion
  559.3 4.0 while.3
  559.3 0.6 fusion.29
  559.9 1.4 bitcast_dynamic-update-slice_fusion.5
  561.3 0.6 fusion.29
  561.9 1.4 bitcast_dynamic-update-slice_fusion.5
  563.3 19.7 %custom-call.15 = f32[2,128,128]{1,2,0:T(8,128)S(1)} custom-call(f32[2,128,128]{2,1,0:T(8,128)S(1)} %get-tuple-element.17), custom_call_target="InvertDiagBlocksLowerTriangular" | custom-call | tf_op jit(solution)/shard_map/triangular_solve | solution.py:33
  582.9 0.3 fusion.4
  583.2 0.3 convolution_subtract_fusion
  583.5 0.3 fusion.2
  583.8 0.8 copy.21
  584.6 0.8 copy.22
  (30 shorter events, 1.0 us)
Async XLA Ops:
  7.2 181.2 %copy-start = (bf16[8,256,256]{2,1,0:T(8,128)(2,1)S(1)}, bf16[8,256,256]{2,1,0:T(8,128)(2,1)}, u32[]{:S(2)}) copy-start(bf16[8,256,256]{2,1,0:T(8,128)(2,1)} %param.6) | copy-start | bytes 3145732
  7.2 164.1 %all-gather.3.cloned.1.call-start = ((), (), s32[]{:S(2)}) async-start(), calls=%async_computation | async-start | bytes 8519680 | tf_op jit(solution)/shard_map/all_gather | solution.py:15
  7.9 238.6 %all-gather.5.cloned.1.call-start = ((), (), s32[]{:S(2)}) async-start(), calls=%async_computation.1 | async-start | bytes 9437184 | tf_op jit(solution)/shard_map/all_gather | solution.py:25
  190.2 2.2 copy-start.1
  194.8 326.3 %all-reduce.4.cloned.1.call-start = ((), (), s32[]{:S(2)}) async-start(), calls=%async_computation.2 | async-start | bytes 524288 | tf_op jit(solution)/shard_map/psum | solution.py:26
Sparse Core Ops, SparseCore 0:
  10.9 160.3 all-gather.2
  194.9 51.5 all-gather.4
  253.3 267.7 all-reduce.3
